TPU v7x, 32 devices: a whole 2x2x4 slice. The times are simulated.
32 devices in a mesh: groups: 2 (over x), graph: 16 (over z, y, core).
Axes of the slice: x: 2, y: 2, z: 4, core: 2. Of those that a mesh axis runs over, the one named last changes fastest.
Arguments:
- edge_state: bfloat16 [32768, 512], P(('groups', 'graph')), parts along dimension 0, may hold values from -6 to 6
- atom_state: bfloat16 [4096, 256], P(('groups', 'graph')), parts along dimension 0, may hold values from -6 to 6
- block_atom: int32 [1024], P(('groups', 'graph')), parts along dimension 0, may hold values from 0 to 127, as said below
- target_row: int32 [32768], P(('groups', 'graph')), parts along dimension 0, may hold values from 0 to 15
- reverse_block: int32 [1024], P(('groups', 'graph')), parts along dimension 0, may hold values from 0 to 511, as said below
- reverse_lane: int32 [32768], P(('groups', 'graph')), parts along dimension 0, may hold values from 0 to 31, as said below
- source_atom: int32 [32768], P(('groups', 'graph')), parts along dimension 0, may hold values from 0 to 127, as said below
- edge_weights: bfloat16 [2, 4, 512, 512], replicated, may hold values from -0.25 to 0.25
- atom_in_weights: bfloat16 [2, 2, 256, 512], replicated, may hold values from -0.375 to 0.375
- atom_out_weights: bfloat16 [2, 512, 256], replicated, may hold values from -0.25 to 0.25
Outputs:
- edge_out: bfloat16 [32768, 512], P(('groups', 'graph')), parts along dimension 0
- atom_out: bfloat16 [4096, 256], P(('groups', 'graph')), parts along dimension 0
There are 2 independent parts, one for each index of `groups`. A program takes and returns all parts, laid end to end along the dimension named above; an argument that names none is the same for every part. Nothing has to cross between parts.
Inputs may be any that keep to these rules, and one draw needn't show every extreme that they name: `block_atom`: among the 32 edge blocks of one device, at most 4 name atom blocks held by any one device (device k holds atom blocks k * 8 to (k + 1) * 8 - 1), and for every device some one device is named exactly 4 times. `reverse_block`: an involution without fixed points. The partner of a block of device k lies on device k - 1, k or k + 1 (no wrap); every device but the last has exactly 8 blocks paired with the device above, every device but the first exactly 8 paired with the device below. `reverse_lane`: together with reverse_block, the map from an edge to its reverse edge is an involution. `source_atom`: Non-decreasing over the edges of one device, and every one of the device's 128 atoms is the source of at least one of its edges.
All inputs are finite; a program needn't handle non-finite values.
Results may differ from a plain program's by a relative error of at most 0.019.
Values may be sent and summed in bfloat16 or wider, within the bound.
A program may use at most 64 MiB of HBM per device.

v0:
```python
import jax
import jax.numpy as jnp
from jax import lax
from jax.sharding import PartitionSpec as P

NB = 32
ATB = 16
CAP = 4
LAYERS = 2
EBLK_DEV = 32
A_DEV = 128
ABLK_DEV = 8


def padded(cells, sides, width):
    for axis, dim in sides:
        count = lax.axis_size(axis)
        ends = count - 1
        head = lax.slice_in_dim(cells, 0, width, axis=dim)
        tail = lax.slice_in_dim(cells, cells.shape[dim] - width, cells.shape[dim], axis=dim)
        cells = jnp.concatenate(
            [
                lax.ppermute(tail, axis, [(i, (i + 1) % count) for i in range(ends)]),
                cells,
                lax.ppermute(head, axis, [((i + 1) % count, i) for i in range(ends)]),
            ],
            axis=dim,
        )
    return cells


def rank_among(order_values, labels, marked):
    earlier = (
        (labels[None, :] == labels[:, None])
        & (order_values[None, :] < order_values[:, None])
        & marked[None, :]
    )
    return jnp.sum(earlier.astype(jnp.int32), axis=1)


def local(
    edge_state,
    atom_state,
    block_atom,
    target_row,
    reverse_block,
    reverse_lane,
    source_atom,
    edge_weights,
    atom_in_weights,
    atom_out_weights,
):
    peers = lax.axis_size("graph")
    device_index = lax.axis_index("graph")
    edge_width = edge_state.shape[1]
    atom_width = atom_state.shape[1]
    position = jnp.arange(EBLK_DEV, dtype=jnp.int32)
    row_start = (position * ATB)[:, None] + target_row.reshape(EBLK_DEV, NB)
    owner = block_atom // ABLK_DEV
    local_block = block_atom - owner * ABLK_DEV
    slot_rank = rank_among(position, owner, jnp.ones((EBLK_DEV,), jnp.bool_))
    slot_index = owner * CAP + slot_rank
    wanted = (
        jnp.zeros((peers * CAP,), jnp.int32).at[slot_index].set(local_block).reshape(peers, CAP)
    )
    asked = lax.all_to_all(wanted, "graph", split_axis=0, concat_axis=0, tiled=True)
    partner_owner = reverse_block // EBLK_DEV
    partner_local = reverse_block - partner_owner * EBLK_DEV
    lane_index = reverse_lane.reshape(EBLK_DEV, NB)
    segment_hot = (jnp.arange(A_DEV, dtype=jnp.int32)[:, None] == source_atom[None, :]).astype(
        jnp.bfloat16
    )
    edges_now = edge_state
    atoms_now = atom_state
    for layer_index in range(LAYERS):
        blocks_here = atoms_now.reshape(ABLK_DEV, ATB, atom_width)
        outgoing = blocks_here[asked]
        incoming = lax.all_to_all(outgoing, "graph", split_axis=0, concat_axis=0, tiled=True)
        chosen = incoming.reshape(peers * CAP, ATB, atom_width)[slot_index]
        rows = chosen.reshape(EBLK_DEV * ATB, atom_width)[row_start.reshape(-1)]
        source_rows = atoms_now[source_atom]
        mixed = jnp.dot(edges_now, edge_weights[layer_index, 0], preferred_element_type=jnp.float32)
        mixed = mixed + jnp.dot(
            rows, atom_in_weights[layer_index, 0], preferred_element_type=jnp.float32
        )
        mixed = mixed + jnp.dot(
            source_rows, atom_in_weights[layer_index, 1], preferred_element_type=jnp.float32
        )
        hidden = jax.nn.silu(mixed).astype(jnp.bfloat16)
        updated = (
            edges_now.astype(jnp.float32)
            + jnp.dot(hidden, edge_weights[layer_index, 1], preferred_element_type=jnp.float32)
        ).astype(jnp.bfloat16)
        blocks_now = updated.reshape(EBLK_DEV, NB, edge_width)
        pool = padded(blocks_now, (("graph", 0),), EBLK_DEV)
        pick = (partner_owner - device_index + 1) * EBLK_DEV + partner_local
        flat_rows = (pick * NB)[:, None] + lane_index
        partner = pool.reshape(-1, edge_width)[flat_rows.reshape(-1)]
        paired = (updated.astype(jnp.float32) + partner.astype(jnp.float32)).astype(jnp.bfloat16)
        gated = jax.nn.silu(
            jnp.dot(paired, edge_weights[layer_index, 2], preferred_element_type=jnp.float32)
        ).astype(jnp.bfloat16)
        edges_now = (
            updated.astype(jnp.float32)
            + jnp.dot(gated, edge_weights[layer_index, 3], preferred_element_type=jnp.float32)
        ).astype(jnp.bfloat16)
        summed = jnp.dot(segment_hot, edges_now, preferred_element_type=jnp.float32)
        pooled = (0.35 * summed).astype(jnp.bfloat16)
        atoms_now = (
            atoms_now.astype(jnp.float32)
            + jax.nn.silu(
                jnp.dot(pooled, atom_out_weights[layer_index], preferred_element_type=jnp.float32)
            )
        ).astype(jnp.bfloat16)
    return (edges_now, atoms_now)


def solution(mesh):
    in_specs = (
        P(("groups", "graph"), None),
        P(("groups", "graph"), None),
        P(("groups", "graph")),
        P(("groups", "graph")),
        P(("groups", "graph")),
        P(("groups", "graph")),
        P(("groups", "graph")),
        P(),
        P(),
        P(),
    )
    out_specs = (P(("groups", "graph"), None), P(("groups", "graph"), None))
    return jax.shard_map(local, mesh=mesh, in_specs=in_specs, out_specs=out_specs, check_vma=False)
```

profile of v0, /device:TPU:9, one launch (start us, length us, event | category | flops | bytes accessed | tf_op | source)
XLA Modules:
  0.0 155.5 jit_solution(15204996502099690308)
XLA Ops:
  0.7 0.7 multiply_subtract_fusion
  1.4 0.2 convert_reduce_fusion
  1.5 0.7 scatter_custom_fusion
  2.2 0.1 all_to_all.14
  2.3 11.1 %all_to_all.22 = s32[16,1,4]{2,1,0:T(1,128)S(1)} all-to-all(s32[16,1,4]{2,1,0:T(1,128)S(1)} %bitcast.90), channel_id=1, replica_groups=mesh['groups'=2,'graph'=16] {'graph'}, dimensions={0} | all-to-all | bytes 512 | tf_op jit(solution)/shard_map/all_to_all | solution.py:66
  13.4 0.1 copy.20
  13.5 0.1 copy.21
  13.6 0.1 reshape.94
  13.7 2.2 %gather_fusion = bf16[64,16,256]{2,1,0:T(8,128)(2,1)} fusion(bf16[8,16,256]{2,1,0:T(8,128)(2,1)} %bitcast.76, s32[1024]{0:T(1024)S(1)} %pad_clamp_fusion.1), kind=kCustom, calls=%fused_computation | custom fusion | bytes 1048832 | tf_op jit(solution)/shard_map/gather | solution.py:77
  15.9 5.2 %all-to-all-start.1 = ((bf16[16,4,16,256]{3,2,1,0:T(8,128)(2,1)}), bf16[16,4,16,256]{3,2,1,0:T(8,128)(2,1)S(1)}, u32[]{:S(2)}, u32[]{:S(2)}) async-start(bf16[16,4,16,256]{3,2,1,0:T(8,128)(2,1)} %bitcast.4), calls=%async_computation.1 | async-start | bytes 1048576 | tf_op jit(solution)/shard_map/all_to_all | solution.py:78
  21.1 0.1 add.126
  21.2 0.1 add.127
  21.3 0.0 copy-start.4
  21.3 3.9 %gather_fusion.3 = bf16[1024,256]{1,0:T(8,128)(2,1)S(1)} fusion(bf16[128,256]{1,0:T(8,128)(2,1)S(1)} %copy-done, s32[1024]{0:T(1024)S(1)} %fusion.76), kind=kCustom, calls=%fused_computation.3 | custom fusion | bytes 1052672 | tf_op jit(solution)/shard_map/gather | solution.py:81
  25.3 2.1 %fusion.34 = f32[1024,512]{1,0:T(8,128)S(1)} fusion(bf16[1024,512]{1,0:T(8,128)(2,1)} %param.10, bf16[2,4,512,512]{3,2,1,0:T(8,128)(2,1)} %param.17), kind=kOutput, calls=%fused_computation.47 | convolution fusion | flops 536870912 | bytes 3670016 | tf_op jit(solution)/shard_map/dot_general | solution.py:82
  27.3 7.9 %all-to-all-done.1 = bf16[16,4,16,256]{3,2,1,0:T(8,128)(2,1)S(1)} async-done(((bf16[16,4,16,256]{3,2,1,0:T(8,128)(2,1)}), bf16[16,4,16,256]{3,2,1,0:T(8,128)(2,1)S(1)}, u32[]{:S(2)}, u32[]{:S(2)}) %all-to-all-start.1) | async-done | bytes 524320 | tf_op jit(solution)/shard_map/all_to_all | solution.py:78
  35.3 0.6 gather_fusion.1
  35.9 3.9 %gather_fusion.2 = bf16[1024,256]{1,0:T(8,128)(2,1)S(1)} fusion(bf16[512,256]{1,0:T(8,128)(2,1)S(1)} %bitcast.79, s32[1024]{0:T(1024)S(1)} %fusion.75), kind=kCustom, calls=%fused_computation.2 | custom fusion | bytes 1052672 | tf_op jit(solution)/shard_map/gather | solution.py:80
  39.8 2.7 %fusion.54 = f32[1024,512]{1,0:T(8,128)} fusion(bf16[1024,256]{1,0:T(8,128)(2,1)S(1)} %gather_fusion.2, bf16[2,2,256,512]{3,2,1,0:T(8,128)(2,1)} %param.18), kind=kOutput, calls=%fused_computation.64 | convolution fusion | flops 268435456 | bytes 2883584 | tf_op jit(solution)/shard_map/dot_general | solution.py:83
  42.5 4.3 %add_convert_fusion.1 = bf16[1024,512]{1,0:T(8,128)(2,1)} fusion(bf16[1024,512]{1,0:T(8,128)(2,1)} %param.10, f32[1024,512]{1,0:T(8,128)S(1)} %fusion.34, f32[1024,512]{1,0:T(8,128)} %fusion.54, bf16[1024,256]{1,0:T(8,128)(2,1)S(1)} %gather_fusion.3, bf16[2,4,512,512]{3,2,1,0:T(8,128)(2,1)} %param.17, bf16[2,2,256,512]{3,2,1,0:T(8,128)(2,1)} %param.18), kind=kOutput, calls=%fused_computation.25 | convolution fusion | flops 810549248 | bytes 7602176 | tf_op jit(solution)/shard_map/dot_general | solution.py:92
  46.8 1.9 %collective-permute-start.1 = (bf16[32,32,512]{2,1,0:T(8,128)(2,1)}, bf16[32,32,512]{2,1,0:T(8,128)(2,1)S(1)}, u32[]{:S(2)}, u32[]{:S(2)}) collective-permute-start(bf16[32,32,512]{2,1,0:T(8,128)(2,1)} %bitcast.84), channel_id=1, source_target_pairs={{1,0},{2,1},{3,2},{4,3},{5,4},{6,5},{7,6},{8,7},{9,8},{10,9},{11,1... | collective-permute-start | bytes 3145736 | tf_op jit(solution)/shard_map/ppermute | solution.py:25
  48.7 3.6 %collective-permute-start = (bf16[32,32,512]{2,1,0:T(8,128)(2,1)}, bf16[32,32,512]{2,1,0:T(8,128)(2,1)}, u32[]{:S(2)}, u32[]{:S(2)}) collective-permute-start(bf16[32,32,512]{2,1,0:T(8,128)(2,1)} %bitcast.85), channel_id=1, source_target_pairs={{0,1},{1,2},{2,3},{3,4},{4,5},{5,6},{6,7},{7,8},{8,9},{9,10},{10,1... | collective-permute-start | bytes 3145736 | tf_op jit(solution)/shard_map/ppermute | solution.py:23
  52.4 0.1 add.137
  52.5 0.1 add.138
  52.5 21.8 %collective-permute-done.1 = bf16[32,32,512]{2,1,0:T(8,128)(2,1)S(1)} collective-permute-done((bf16[32,32,512]{2,1,0:T(8,128)(2,1)}, bf16[32,32,512]{2,1,0:T(8,128)(2,1)S(1)}, u32[]{:S(2)}, u32[]{:S(2)}) %collective-permute-start.1) | collective-permute-done | bytes 1048608 | tf_op jit(solution)/shard_map/ppermute | solution.py:25
  74.3 1.0 copy-done.2
  75.3 2.0 %pad_maximum_fusion = bf16[96,32,512]{2,1,0:T(8,128)(2,1)S(1)} fusion(bf16[32,32,512]{2,1,0:T(8,128)(2,1)} %copy-done.2, bf16[32,32,512]{2,1,0:T(8,128)(2,1)} %bitcast.86, bf16[32,32,512]{2,1,0:T(8,128)(2,1)} %collective-permute-done), kind=kLoop, calls=%fused_computation.11 | loop fusion | flops 3145728 | bytes 6291456 | tf_op jit(solution)/shard_map/concatenate | solution.py:21
  77.4 5.1 %gather_fusion.4 = bf16[1024,512]{1,0:T(8,128)(2,1)} fusion(bf16[3072,512]{1,0:T(8,128)(2,1)S(1)} %bitcast.81, s32[1024]{0:T(1024)S(1)} %fusion.77), kind=kCustom, calls=%fused_computation.4 | custom fusion | bytes 2101248 | tf_op jit(solution)/shard_map/gather | solution.py:98
  82.5 3.6 %fusion.1 = bf16[1024,512]{1,0:T(8,128)(2,1)S(1)} fusion(bf16[1024,512]{1,0:T(8,128)(2,1)} %add_convert_fusion.1, bf16[1024,512]{1,0:T(8,128)(2,1)} %gather_fusion.4, bf16[2,4,512,512]{3,2,1,0:T(8,128)(2,1)} %param.17), kind=kOutput, calls=%fused_computation.18 | convolution fusion | flops 1080033280 | bytes 5242880 | tf_op jit(solution)/shard_map/dot_general | solution.py:105
  86.1 0.0 copy-start.1
  86.1 0.5 add_convert_fusion.3
  86.6 1.4 gather_fusion.5
  88.0 4.0 %all-to-all-start.2 = ((bf16[16,4,16,256]{3,2,1,0:T(8,128)(2,1)}), bf16[16,4,16,256]{3,2,1,0:T(8,128)(2,1)S(1)}, u32[]{:S(2)}, u32[]{:S(2)}) async-start(bf16[16,4,16,256]{3,2,1,0:T(8,128)(2,1)} %bitcast.17), calls=%async_computation.2 | async-start | bytes 1048576 | tf_op jit(solution)/shard_map/all_to_all | solution.py:78
  92.0 4.9 %gather_fusion.8 = bf16[1024,256]{1,0:T(8,128)(2,1)} fusion(bf16[128,256]{1,0:T(8,128)(2,1)S(1)} %add_convert_fusion.3, s32[1024]{0:T(1024)S(1)} %fusion.76), kind=kCustom, calls=%fused_computation.8 | custom fusion | bytes 1052672 | tf_op jit(solution)/shard_map/gather | solution.py:81
  97.0 2.1 %fusion.28 = f32[1024,512]{1,0:T(8,128)S(1)} fusion(bf16[1024,512]{1,0:T(8,128)(2,1)} %copy-done.1, bf16[2,4,512,512]{3,2,1,0:T(8,128)(2,1)} %param.17), kind=kOutput, calls=%fused_computation.42 | convolution fusion | flops 536870912 | bytes 3670016 | tf_op jit(solution)/shard_map/dot_general | solution.py:82
  99.0 7.1 %all-to-all-done.2 = bf16[16,4,16,256]{3,2,1,0:T(8,128)(2,1)S(1)} async-done(((bf16[16,4,16,256]{3,2,1,0:T(8,128)(2,1)}), bf16[16,4,16,256]{3,2,1,0:T(8,128)(2,1)S(1)}, u32[]{:S(2)}, u32[]{:S(2)}) %all-to-all-start.2) | async-done | bytes 524320 | tf_op jit(solution)/shard_map/all_to_all | solution.py:78
  106.2 0.6 gather_fusion.6
  106.7 3.9 %gather_fusion.7 = bf16[1024,256]{1,0:T(8,128)(2,1)S(1)} fusion(bf16[512,256]{1,0:T(8,128)(2,1)S(1)} %bitcast.78, s32[1024]{0:T(1024)S(1)} %fusion.75), kind=kCustom, calls=%fused_computation.7 | custom fusion | bytes 1052672 | tf_op jit(solution)/shard_map/gather | solution.py:80
  110.7 2.7 %fusion.49 = f32[1024,512]{1,0:T(8,128)} fusion(bf16[1024,256]{1,0:T(8,128)(2,1)S(1)} %gather_fusion.7, bf16[2,2,256,512]{3,2,1,0:T(8,128)(2,1)} %param.18), kind=kOutput, calls=%fused_computation.60 | convolution fusion | flops 268435456 | bytes 2883584 | tf_op jit(solution)/shard_map/dot_general | solution.py:83
  113.4 3.4 %add_convert_fusion = bf16[1024,512]{1,0:T(8,128)(2,1)S(1)} fusion(bf16[1024,512]{1,0:T(8,128)(2,1)} %copy-done.1, f32[1024,512]{1,0:T(8,128)S(1)} %fusion.28, f32[1024,512]{1,0:T(8,128)} %fusion.49, bf16[1024,256]{1,0:T(8,128)(2,1)} %gather_fusion.8, bf16[2,4,512,512]{3,2,1,0:T(8,128)(2,1)} %param.17, bf16[2,2,256,512]{3,2,1,0:T(8,128)(2,1)} %param.18), kind=kOutput, calls=%fused_computation.22 | convolution fusion | flops 810549248 | bytes 7602176 | tf_op jit(solution)/shard_map/dot_general | solution.py:92
  116.8 0.0 copy-start.3
  116.8 1.9 %collective-permute-start.3 = (bf16[32,32,512]{2,1,0:T(8,128)(2,1)S(1)}, bf16[32,32,512]{2,1,0:T(8,128)(2,1)S(1)}, u32[]{:S(2)}, u32[]{:S(2)}) collective-permute-start(bf16[32,32,512]{2,1,0:T(8,128)(2,1)S(1)} %bitcast.87), channel_id=1, source_target_pairs={{1,0},{2,1},{3,2},{4,3},{5,4},{6,5},{7,6},{8,7},{9,8},{10,9},{11,1... | collective-permute-start | bytes 3145736 | tf_op jit(solution)/shard_map/ppermute | solution.py:25
  118.8 3.6 %collective-permute-start.2 = (bf16[32,32,512]{2,1,0:T(8,128)(2,1)S(1)}, bf16[32,32,512]{2,1,0:T(8,128)(2,1)S(1)}, u32[]{:S(2)}, u32[]{:S(2)}) collective-permute-start(bf16[32,32,512]{2,1,0:T(8,128)(2,1)S(1)} %bitcast.88), channel_id=1, source_target_pairs={{0,1},{1,2},{2,3},{3,4},{4,5},{5,6},{6,7},{7,8},{8,9},{9,10},{10,1... | collective-permute-start | bytes 3145736 | tf_op jit(solution)/shard_map/ppermute | solution.py:23
  122.4 21.8 %collective-permute-done.3 = bf16[32,32,512]{2,1,0:T(8,128)(2,1)S(1)} collective-permute-done((bf16[32,32,512]{2,1,0:T(8,128)(2,1)S(1)}, bf16[32,32,512]{2,1,0:T(8,128)(2,1)S(1)}, u32[]{:S(2)}, u32[]{:S(2)}) %collective-permute-start.3) | collective-permute-done | bytes 1048608 | tf_op jit(solution)/shard_map/ppermute | solution.py:25
  144.2 1.4 pad_maximum_fusion.1
  145.6 5.1 %gather_fusion.9 = bf16[1024,512]{1,0:T(8,128)(2,1)} fusion(bf16[3072,512]{1,0:T(8,128)(2,1)S(1)} %bitcast.80, s32[1024]{0:T(1024)S(1)} %fusion.77), kind=kCustom, calls=%fused_computation.9 | custom fusion | bytes 2101248 | tf_op jit(solution)/shard_map/gather | solution.py:98
  150.7 3.6 %fusion.3 = bf16[1024,512]{1,0:T(8,128)(2,1)S(1)} fusion(bf16[1024,512]{1,0:T(8,128)(2,1)} %copy-done.3, bf16[1024,512]{1,0:T(8,128)(2,1)} %gather_fusion.9, bf16[2,4,512,512]{3,2,1,0:T(8,128)(2,1)} %param.17), kind=kOutput, calls=%fused_computation.20 | convolution fusion | flops 1080033280 | bytes 5242880 | tf_op jit(solution)/shard_map/dot_general | solution.py:105
  154.4 1.1 add_convert_fusion.2
  (29 shorter events, 0.1 us)
Async XLA Ops:
  0.6 20.6 %copy-start = (bf16[128,256]{1,0:T(8,128)(2,1)S(1)}, bf16[128,256]{1,0:T(8,128)(2,1)}, u32[]{:S(2)}) copy-start(bf16[128,256]{1,0:T(8,128)(2,1)} %param.11) | copy-start | bytes 196612
  0.6 20.6 %copy-start.6 = (s32[1024]{0:T(1024)S(1)}, s32[1024]{0:T(1024)}, u32[]{:S(2)}) copy-start(s32[1024]{0:T(1024)} %param.16) | copy-start | bytes 12292
  15.9 19.4 %all-to-all-start.1 = ((bf16[16,4,16,256]{3,2,1,0:T(8,128)(2,1)}), bf16[16,4,16,256]{3,2,1,0:T(8,128)(2,1)S(1)}, u32[]{:S(2)}, u32[]{:S(2)}) async-start(bf16[16,4,16,256]{3,2,1,0:T(8,128)(2,1)} %bitcast.4), calls=%async_computation.1 | async-start | bytes 1048576 | tf_op jit(solution)/shard_map/all_to_all | solution.py:78
  21.3 4.0 %copy-start.4 = (s32[1024]{0:T(1024)S(1)}, s32[1024]{0:T(1024)}, u32[]{:S(2)}) copy-start(s32[1024]{0:T(1024)} %param.13) | copy-start | bytes 12292
  42.5 9.8 %copy-start.9 = (s32[32]{0:T(128)S(1)}, s32[32]{0:T(128)}, u32[]{:S(2)}) copy-start(s32[32]{0:T(128)} %param.14) | copy-start | bytes 388
  42.5 10.0 %copy-start.5 = (s32[1024]{0:T(1024)S(1)}, s32[1024]{0:T(1024)}, u32[]{:S(2)}) copy-start(s32[1024]{0:T(1024)} %param.15) | copy-start | bytes 12292
  46.8 27.6 %collective-permute-start.1 = (bf16[32,32,512]{2,1,0:T(8,128)(2,1)}, bf16[32,32,512]{2,1,0:T(8,128)(2,1)S(1)}, u32[]{:S(2)}, u32[]{:S(2)}) collective-permute-start(bf16[32,32,512]{2,1,0:T(8,128)(2,1)} %bitcast.84), channel_id=1, source_target_pairs={{1,0},{2,1},{3,2},{4,3},{5,4},{6,5},{7,6},{8,7},{9,8},{10,9},{11,1... | collective-permute-start | bytes 3145736 | tf_op jit(solution)/shard_map/ppermute | solution.py:25
  48.7 26.6 %collective-permute-start = (bf16[32,32,512]{2,1,0:T(8,128)(2,1)}, bf16[32,32,512]{2,1,0:T(8,128)(2,1)}, u32[]{:S(2)}, u32[]{:S(2)}) collective-permute-start(bf16[32,32,512]{2,1,0:T(8,128)(2,1)} %bitcast.85), channel_id=1, source_target_pairs={{0,1},{1,2},{2,3},{3,4},{4,5},{5,6},{6,7},{7,8},{8,9},{9,10},{10,1... | collective-permute-start | bytes 3145736 | tf_op jit(solution)/shard_map/ppermute | solution.py:23
  74.3 1.0 copy-start.2
  82.5 3.7 %copy-start.7 = (bf16[2,512,256]{2,1,0:T(8,128)(2,1)S(1)}, bf16[2,512,256]{2,1,0:T(8,128)(2,1)}, u32[]{:S(2)}) copy-start(bf16[2,512,256]{2,1,0:T(8,128)(2,1)} %param.19) | copy-start | bytes 1572868
  86.1 1.9 %copy-start.1 = (bf16[1024,512]{1,0:T(8,128)(2,1)}, bf16[1024,512]{1,0:T(8,128)(2,1)S(1)}, u32[]{:S(2)}) copy-start(bf16[1024,512]{1,0:T(8,128)(2,1)S(1)} %fusion.1) | copy-start | bytes 3145732
  88.0 18.1 %all-to-all-start.2 = ((bf16[16,4,16,256]{3,2,1,0:T(8,128)(2,1)}), bf16[16,4,16,256]{3,2,1,0:T(8,128)(2,1)S(1)}, u32[]{:S(2)}, u32[]{:S(2)}) async-start(bf16[16,4,16,256]{3,2,1,0:T(8,128)(2,1)} %bitcast.17), calls=%async_computation.2 | async-start | bytes 1048576 | tf_op jit(solution)/shard_map/all_to_all | solution.py:78
  116.8 27.4 %copy-start.3 = (bf16[1024,512]{1,0:T(8,128)(2,1)}, bf16[1024,512]{1,0:T(8,128)(2,1)S(1)}, u32[]{:S(2)}) copy-start(bf16[1024,512]{1,0:T(8,128)(2,1)S(1)} %add_convert_fusion) | copy-start | bytes 3145732
  116.8 27.4 %collective-permute-start.3 = (bf16[32,32,512]{2,1,0:T(8,128)(2,1)S(1)}, bf16[32,32,512]{2,1,0:T(8,128)(2,1)S(1)}, u32[]{:S(2)}, u32[]{:S(2)}) collective-permute-start(bf16[32,32,512]{2,1,0:T(8,128)(2,1)S(1)} %bitcast.87), channel_id=1, source_target_pairs={{1,0},{2,1},{3,2},{4,3},{5,4},{6,5},{7,6},{8,7},{9,8},{10,9},{11,1... | collective-permute-start | bytes 3145736 | tf_op jit(solution)/shard_map/ppermute | solution.py:25
  118.8 25.4 %collective-permute-start.2 = (bf16[32,32,512]{2,1,0:T(8,128)(2,1)S(1)}, bf16[32,32,512]{2,1,0:T(8,128)(2,1)S(1)}, u32[]{:S(2)}, u32[]{:S(2)}) collective-permute-start(bf16[32,32,512]{2,1,0:T(8,128)(2,1)S(1)} %bitcast.88), channel_id=1, source_target_pairs={{0,1},{1,2},{2,3},{3,4},{4,5},{5,6},{6,7},{7,8},{8,9},{9,10},{10,1... | collective-permute-start | bytes 3145736 | tf_op jit(solution)/shard_map/ppermute | solution.py:23
  150.7 3.7 %copy-start.8 = (bf16[2,512,256]{2,1,0:T(8,128)(2,1)S(1)}, bf16[2,512,256]{2,1,0:T(8,128)(2,1)}, u32[]{:S(2)}) copy-start(bf16[2,512,256]{2,1,0:T(8,128)(2,1)} %param.19) | copy-start | bytes 1572868
  154.4 1.1 copy-start.10
where the time goes:
time: 157 us; the launch traced here: 156 us
  waiting for transfers between devices  58.6 us (37%)
  local copies, waits for them, and re-layouts  34 us (22%)
  matrix products  26.1 us (17%)
  starting transfers between devices  20.3 us (13%)
  blocking collectives  11.1 us (7%)
  other arithmetic  4.41 us (3%)
    ppermute x2, waiting for transfers between devices, padded(): lax.ppermute(head, axis, [((i + 1) % count, i) for i in range(ends)])  43.6 us
    all_to_all x2, waiting for transfers between devices, local(): lax.all_to_all(outgoing, 'graph', split_axis=0, concat_axis=0, tiled=True)  15.1 us
    all_to_all x1, blocking collectives, local(): lax.all_to_all(wanted, 'graph', split_axis=0, concat_axis=0, tiled=True)  11.1 us
    gather x2, local copies, waits for them, and re-layouts, local(): partner = pool.reshape(-1, edge_width)[flat_rows.reshape(-1)]  10.2 us
    all_to_all x2, starting transfers between devices, local(): lax.all_to_all(outgoing, 'graph', split_axis=0, concat_axis=0, tiled=True)  9.2 us
    gather x2, local copies, waits for them, and re-layouts, local(): source_rows = atoms_now[source_atom]  8.89 us
    gather x2, local copies, waits for them, and re-layouts, local(): rows = chosen.reshape(EBLK_DEV * ATB, atom_width)[row_start.reshape(-1)]  7.88 us
    dot_general x2, matrix products, local(): jnp.dot(hidden, edge_weights[layer_index, 1], preferred_element_type=jnp....  7.69 us
  transfers between devices with their start and end apart: 6, of which 4 were waited for; matrix products, arithmetic and copies ran while one was open for 9% of the time, Pallas kernels for 0%

commit v1 on v0

v1 whole, which is shorter than its diff:
```python
import functools

import jax
import jax.numpy as jnp
from jax import lax
from jax.experimental import pallas as pl
from jax.experimental.pallas import tpu as pltpu
from jax.sharding import PartitionSpec as P

NB = 32
ATB = 16
LAYERS = 2
EBLK = 32
A_DEV = 128
QUARTER = 8
CH = QUARTER * NB
MESH = pl.DeviceIdType.MESH
F32 = jnp.float32
BF16 = jnp.bfloat16


def dot(a, b):
    return jnp.dot(a, b, preferred_element_type=F32)


def silu(v):
    return (0.5 * v) * (1.0 + jnp.tanh(0.5 * v))


def hot(mask):
    return jnp.where(mask, 1.0, 0.0).astype(BF16)


def kernel(
    n,
    rblock,
    batom,
    edge_hbm,
    atom_in,
    trow,
    rlane,
    satom,
    ew_hbm,
    aw_hbm,
    ow_hbm,
    edge_out,
    atom_out,
    pos_out,
    raw,
    ohe,
    edges,
    upd,
    part,
    oht,
    ohs,
    ohr,
    ohc,
    table,
    recv_up,
    recv_dn,
    ew,
    aw,
    ow,
    load_sem,
    out_sem,
    ag_send,
    ag_recv,
    x_send,
    x_recv,
):
    me = lax.axis_index("graph")
    planes = n // 4
    y = (me // 2) % 2
    c = me % 2
    y_peer = me + 2 - 4 * y
    s_peer = me + 1 - 2 * c
    s_y_peer = s_peer + 2 - 4 * y
    has_up = me < n - 1
    has_dn = me > 0

    loads = [pltpu.make_async_copy(edge_hbm, raw, load_sem.at[0])]
    order = [(aw_hbm, aw, 0), (ew_hbm, ew, 0), (ow_hbm, ow, 0), (aw_hbm, aw, 1), (ew_hbm, ew, 1), (ow_hbm, ow, 1)]
    for i, (src, dst, l) in enumerate(order):
        loads.append(pltpu.make_async_copy(src.at[l], dst.at[l], load_sem.at[i + 1]))
    for cp in loads:
        cp.start()

    barrier = pltpu.get_barrier_semaphore()

    def greet(dev):
        pl.semaphore_signal(barrier, inc=1, device_id={"graph": dev}, device_id_type=MESH)

    for d in range(1, planes):
        greet((me + 4 * d) % n)
    greet(y_peer)
    greet(s_peer)

    greet((me + n + 2 * c - 1) % n)
    pl.semaphore_wait(barrier, planes + 2)

    def shard_rows(dev):
        return pl.ds(pl.multiple_of(dev * A_DEV, A_DEV), A_DEV)

    sent = []

    def push(l, shard, dev):
        rows = shard_rows(shard)
        cp = pltpu.make_async_remote_copy(
            src_ref=table.at[l, rows],
            dst_ref=table.at[l, rows],
            send_sem=ag_send.at[l, len(sent) % (4 * planes)],
            recv_sem=ag_recv.at[l, shard],
            device_id={"graph": dev},
            device_id_type=MESH,
        )
        cp.start()
        sent.append(cp)

    def arrived(l, shard):
        rows = shard_rows(shard)
        pltpu.make_async_remote_copy(
            src_ref=table.at[l, rows],
            dst_ref=table.at[l, rows],
            send_sem=ag_send.at[l, 0],
            recv_sem=ag_recv.at[l, shard],
            device_id={"graph": s_peer},
            device_id_type=MESH,
        ).wait_recv()

    def exchange(l, up):
        return pltpu.make_async_remote_copy(
            src_ref=upd.at[pl.ds(0 if up else CH, CH)],
            dst_ref=recv_dn.at[l] if up else recv_up.at[l],
            send_sem=x_send.at[l, 0 if up else 1],
            recv_sem=x_recv.at[l, 0 if up else 1],
            device_id={"graph": me + 1 if up else me - 1},
            device_id_type=MESH,
        )

    def block_order(key, is_up, is_dn, rank):
        n_up = jnp.where(has_up, QUARTER, 0)
        inner = rank - n_up - jnp.where(has_dn, QUARTER, 0)
        first_base = jnp.where(has_dn, jnp.where(has_up, 2 * QUARTER, 0), QUARTER)
        later_base = jnp.where(has_dn, jnp.where(has_up, 2 * QUARTER, QUARTER), QUARTER)
        inner = jnp.where(inner < QUARTER, inner + first_base, inner + later_base)
        return jnp.where(is_up, rank, jnp.where(is_dn, QUARTER + rank - n_up, inner))

    def prepare():
        square = (EBLK, EBLK)
        lanes = lax.broadcasted_iota(jnp.int32, square, 1)
        subs = lax.broadcasted_iota(jnp.int32, square, 0)
        rb = jnp.broadcast_to(rblock[...], square)
        low = me * EBLK
        is_up = rb >= low + EBLK
        is_dn = rb < low
        mine = lanes + low
        inner_key = 2 * jnp.minimum(mine, rb) + jnp.where(mine > rb, 1, 0)
        big = 4 * n * EBLK
        key = jnp.where(is_up, lanes, jnp.where(is_dn, big + rb, 2 * big + inner_key))
        rank = jnp.sum(jnp.where(key.T < key, 1, 0), axis=0, keepdims=True)
        pos = block_order(key, is_up, is_dn, jnp.broadcast_to(rank, square))
        pos_out[...] = pos[0:1, :]
        here = pos == subs
        pcol = jnp.sum(jnp.where(here, lanes, 0), axis=1, keepdims=True)
        bcol = jnp.sum(jnp.where(here, jnp.broadcast_to(batom[...], square), 0), axis=1, keepdims=True)
        pick = jnp.where(here, 1.0, 0.0).astype(BF16)

        def by_slot(ref):
            return dot(pick, ref[...].astype(F32).astype(BF16)).T.astype(jnp.int32)

        tcol = by_slot(trow)
        scol = by_slot(satom)
        rcol = by_slot(rlane)
        wide = lax.broadcasted_iota(jnp.int32, (NB, CH), 1)
        narrow = lax.broadcasted_iota(jnp.int32, (NB, A_DEV), 1)
        for p in range(EBLK):
            rows = pl.ds(p * NB, NB)
            oht[rows, :] = hot(wide == tcol[:, p : p + 1] + (p % 16) * ATB)
            ohs[rows, :] = hot(narrow == scol[:, p : p + 1])
            slot = p % QUARTER
            swapped = (slot ^ 1) * NB
            if p < 2 * QUARTER:
                remote = has_up if p < QUARTER else has_dn
                off = jnp.where(remote, slot * NB, swapped)
            else:
                off = swapped
            ohr[rows, :] = hot(wide == rcol[:, p : p + 1] + off)
        e_dev = raw.shape[0]
        from_edge = lax.broadcasted_iota(jnp.int32, (NB, e_dev), 1) - lax.broadcasted_iota(jnp.int32, (NB, e_dev), 0)
        for p in range(EBLK):
            ohe[pl.ds(p * NB, NB), :] = hot(from_edge == pcol[p : p + 1, :] * NB)
        atoms_all = n * A_DEV
        from_atom = lax.broadcasted_iota(jnp.int32, (ATB, atoms_all), 1) - lax.broadcasted_iota(jnp.int32, (ATB, atoms_all), 0)
        for p in range(EBLK):
            ohc[pl.ds(p * ATB, ATB), :] = hot(from_atom == bcol[p : p + 1, :] * ATB)

    def sort_edges():
        loads[0].wait()
        for q in range(4):
            rows = pl.ds(q * CH, CH)
            edges[rows, :] = dot(ohe[rows, :], raw[...]).astype(BF16)

    def result(q):
        rows = pl.ds(q * CH, CH)
        return pltpu.make_async_copy(edges.at[rows], edge_out.at[rows], out_sem.at[q])

    for l in range(LAYERS):
        atoms = atom_in if l == 0 else atom_out
        del sent[:]
        table[l, shard_rows(me), :] = atoms[...]
        for d in range(1, planes):
            push(l, me, (me + 4 * d) % n)
        push(l, me, y_peer)
        push(l, me, s_peer)

        if l == 0:
            prepare()
        for d in range(1, planes):
            shard = (me + n - 4 * d) % n
            arrived(l, shard)
            push(l, shard, y_peer)
            push(l, shard, s_peer)
        if l == 0:
            sort_edges()
            loads[1].wait()
            loads[2].wait()
        for d in range(planes):
            shard = (y_peer + n - 4 * d) % n
            arrived(l, shard)
            push(l, shard, s_peer)

        sproj = dot(atoms[...], aw[l, 1]).astype(BF16)
        for q in range(4):
            rows = pl.ds(q * CH, CH)
            part[rows, :] = dot(edges[rows, :], ew[l, 0]) + dot(ohs[rows, :], sproj)

        for d in range(planes):
            arrived(l, (s_peer + n - 4 * d) % n)
            arrived(l, (s_y_peer + n - 4 * d) % n)

        def project(half):
            chosen = dot(ohc[pl.ds(half * CH, CH), :], table[l]).astype(BF16)
            return dot(chosen, aw[l, 0]).astype(BF16)

        def first(q):
            rows = pl.ds(q * CH, CH)
            h = silu(part[rows, :] + dot(oht[rows, :], tproj)).astype(BF16)
            upd[rows, :] = (edges[rows, :].astype(F32) + dot(h, ew[l, 1])).astype(BF16)

        tproj = project(0)
        first(0)

        @pl.when(has_up)
        def _():
            exchange(l, True).start()

        first(1)

        @pl.when(has_dn)
        def _():
            exchange(l, False).start()

        tproj = project(1)
        first(2)
        first(3)

        if l == 0:
            loads[3].wait()

        def second(q, partner):
            rows = pl.ds(q * CH, CH)
            u = upd[rows, :].astype(F32)
            paired = (u + dot(ohr[rows, :], partner)).astype(BF16)
            g = silu(dot(paired, ew[l, 2])).astype(BF16)
            e = (u + dot(g, ew[l, 3])).astype(BF16)
            edges[rows, :] = e
            if l == LAYERS - 1:
                result(q).start()
            return lax.dot_general(ohs[rows, :], e, (((0,), (0,)), ((), ())), preferred_element_type=F32)

        summed = second(2, upd[pl.ds(2 * CH, CH), :])
        summed = summed + second(3, upd[pl.ds(3 * CH, CH), :])

        @pl.when(has_up)
        def _():
            exchange(l, False).wait_recv()

        @pl.when(jnp.logical_not(has_up))
        def _():
            recv_up[l] = upd[pl.ds(0, CH), :]

        summed = summed + second(0, recv_up[l])

        @pl.when(has_dn)
        def _():
            exchange(l, True).wait_recv()

        @pl.when(jnp.logical_not(has_dn))
        def _():
            recv_dn[l] = upd[pl.ds(CH, CH), :]

        summed = summed + second(1, recv_dn[l])

        pooled = (0.35 * summed).astype(BF16)
        atom_out[...] = (atoms[...].astype(F32) + silu(dot(pooled, ow[l]))).astype(BF16)

        for cp in sent:
            cp.wait_send()

        @pl.when(has_up)
        def _():
            exchange(l, True).wait_send()

        @pl.when(has_dn)
        def _():
            exchange(l, False).wait_send()

        if l == 0:
            for cp in loads[4:]:
                cp.wait()

    for q in range(4):
        result(q).wait()


def unsort(pos, src, dst, sem):
    for b in range(EBLK):
        start = pl.multiple_of(pos[0, b] * NB, NB)
        pltpu.make_async_copy(src.at[pl.ds(start, NB)], dst.at[pl.ds(b * NB, NB)], sem).start()
    pltpu.make_async_copy(src, dst, sem).wait()


def local(
    n,
    edge_state,
    atom_state,
    block_atom,
    target_row,
    reverse_block,
    reverse_lane,
    source_atom,
    edge_weights,
    atom_in_weights,
    atom_out_weights,
):
    de = edge_state.shape[1]
    da = atom_state.shape[1]
    e_dev = edge_state.shape[0]
    vmem = pl.BlockSpec(memory_space=pltpu.VMEM)
    smem = pl.BlockSpec(memory_space=pltpu.SMEM)
    anys = pl.BlockSpec(memory_space=pl.ANY)
    planes = n // 4
    ordered, atoms, pos = pl.pallas_call(
        functools.partial(kernel, n),
        out_shape=(
            jax.ShapeDtypeStruct((e_dev, de), BF16),
            jax.ShapeDtypeStruct((A_DEV, da), BF16),
            jax.ShapeDtypeStruct((1, EBLK), jnp.int32),
        ),
        in_specs=[vmem, vmem, anys, vmem, vmem, vmem, vmem, anys, anys, anys],
        out_specs=(anys, vmem, vmem),
        scratch_shapes=[
            pltpu.VMEM((e_dev, de), BF16),
            pltpu.VMEM((e_dev, e_dev), BF16),
            pltpu.VMEM((e_dev, de), BF16),
            pltpu.VMEM((e_dev, de), BF16),
            pltpu.VMEM((e_dev, de), F32),
            pltpu.VMEM((e_dev, CH), BF16),
            pltpu.VMEM((e_dev, A_DEV), BF16),
            pltpu.VMEM((e_dev, CH), BF16),
            pltpu.VMEM((EBLK * ATB, n * A_DEV), BF16),
            pltpu.VMEM((LAYERS, n * A_DEV, da), BF16),
            pltpu.VMEM((LAYERS, CH, de), BF16),
            pltpu.VMEM((LAYERS, CH, de), BF16),
            pltpu.VMEM(edge_weights.shape, BF16),
            pltpu.VMEM(atom_in_weights.shape, BF16),
            pltpu.VMEM(atom_out_weights.shape, BF16),
            pltpu.SemaphoreType.DMA((7,)),
            pltpu.SemaphoreType.DMA((4,)),
            pltpu.SemaphoreType.DMA((LAYERS, 4 * planes)),
            pltpu.SemaphoreType.DMA((LAYERS, n)),
            pltpu.SemaphoreType.DMA((LAYERS, 2)),
            pltpu.SemaphoreType.DMA((LAYERS, 2)),
        ],
        compiler_params=pltpu.CompilerParams(
            collective_id=0, has_side_effects=True, vmem_limit_bytes=48 * 1024 * 1024
        ),
    )(
        reverse_block.reshape(1, EBLK),
        block_atom.reshape(1, EBLK),
        edge_state,
        atom_state,
        target_row.reshape(EBLK, NB),
        reverse_lane.reshape(EBLK, NB),
        source_atom.reshape(EBLK, NB),
        edge_weights,
        atom_in_weights,
        atom_out_weights,
    )
    edges = pl.pallas_call(
        unsort,
        out_shape=jax.ShapeDtypeStruct((e_dev, de), BF16),
        in_specs=[smem, anys],
        out_specs=anys,
        scratch_shapes=[pltpu.SemaphoreType.DMA],
    )(pos, ordered)
    return edges, atoms


def solution(mesh):
    both = P(("groups", "graph"))
    rows = P(("groups", "graph"), None)
    return jax.shard_map(
        functools.partial(local, mesh.shape["graph"]),
        mesh=mesh,
        in_specs=(rows, rows, both, both, both, both, both, P(), P(), P()),
        out_specs=(rows, rows),
        check_vma=False,
    )
```

time: 157 us -> 91 us (0.58)
  Pallas kernels: 0 us -> 79.9 us
  waiting for transfers between devices: 58.6 us -> 0 us
  matrix products: 26.1 us -> 0 us
  local copies, waits for them, and re-layouts: 34 us -> 10 us
  starting transfers between devices: 20.3 us -> 0 us
  blocking collectives: 11.1 us -> 0 us
  other arithmetic: 4.41 us -> 0 us
    pallas_call x0 -> x2, Pallas kernels: none -> 79.9 us  [the longest x1 46.4 us: local(): pl.pallas_call(functools.partial(kernel, n), out_shape=(jax.ShapeDtypeStr...]
    ppermute x4 -> x0, waiting for transfers between devices: 43.6 us -> none  [the longest x2 43.6 us: padded(): lax.ppermute(head, axis, [((i + 1) % count, i) for i in range(ends)])]
    gather x10 -> x0, local copies, waits for them, and re-layouts: 31.7 us -> none  [the longest x2 10.2 us: local(): partner = pool.reshape(-1, edge_width)[flat_rows.reshape(-1)]]
    dot_general x10 -> x0, matrix products: 26.1 us -> none  [the longest x2 7.69 us: local(): jnp.dot(hidden, edge_weights[layer_index, 1], preferred_element_type=jnp....]
    all_to_all x2 -> x0, waiting for transfers between devices: 15.1 us -> none  [local(): lax.all_to_all(outgoing, 'graph', split_axis=0, concat_axis=0, tiled=True)]
    ppermute x4 -> x0, starting transfers between devices: 11.1 us -> none  [the longest x2 7.29 us: padded(): lax.ppermute(tail, axis, [(i, (i + 1) % count) for i in range(ends)])]
    all_to_all x1 -> x0, blocking collectives: 11.1 us -> none  [local(): lax.all_to_all(wanted, 'graph', split_axis=0, concat_axis=0, tiled=True)]
    all_to_all x2 -> x0, starting transfers between devices: 9.2 us -> none  [local(): lax.all_to_all(outgoing, 'graph', split_axis=0, concat_axis=0, tiled=True)]
  transfers between devices with their start and end apart: 6 -> 0, of which waited for: 4 -> 0; matrix products, arithmetic and copies ran while one was open for 9% -> 0% of each run, Pallas kernels for 0% -> 0%
where the time goes in v1:
time: 91 us; the launch traced here: 90.6 us
  Pallas kernels  79.9 us (88%)
  local copies, waits for them, and re-layouts  10 us (11%)
    pallas_call x1, Pallas kernels, local(): pl.pallas_call(functools.partial(kernel, n), out_shape=(jax.ShapeDtypeStr...  46.4 us
    pallas_call x1, Pallas kernels, local(): pl.pallas_call(unsort, out_shape=jax.ShapeDtypeStruct((e_dev, de), BF16),...  33.5 us
    unnamed x17, local copies, waits for them, and re-layouts  7.74 us

profile of v1, /device:TPU:9, one launch (start us, length us, event | category | flops | bytes accessed | tf_op | source)
XLA Modules:
  0.0 90.6 jit_solution(8779457953669643581)
XLA Ops:
  0.6 0.8 reshape.21.trow
  1.4 0.8 reshape.22.rlane
  2.1 0.8 reshape.23.satom
  2.9 0.0 copy-start.1
  2.9 1.2 %copy-done.1 = bf16[1024,512]{1,0:T(8,128)(2,1)S(1)} copy-done((bf16[1024,512]{1,0:T(8,128)(2,1)S(1)}, bf16[1024,512]{1,0:T(8,128)(2,1)}, u32[]{:S(2)}) %copy-start.1) | copy-done | bytes 1048600
  4.1 0.0 copy-start.2
  4.1 1.2 %copy-done.2 = bf16[2,2,256,512]{3,2,1,0:T(8,128)(2,1)S(1)} copy-done((bf16[2,2,256,512]{3,2,1,0:T(8,128)(2,1)S(1)}, bf16[2,2,256,512]{3,2,1,0:T(8,128)(2,1)}, u32[]{:S(2)}) %copy-start.2) | copy-done | bytes 1048600
  5.4 0.0 copy-start.3
  5.4 1.0 %copy-done.3 = bf16[2,512,256]{2,1,0:T(8,128)(2,1)S(1)} copy-done((bf16[2,512,256]{2,1,0:T(8,128)(2,1)S(1)}, bf16[2,512,256]{2,1,0:T(8,128)(2,1)}, u32[]{:S(2)}) %copy-start.3) | copy-done | bytes 524312
  6.4 0.0 copy-start.4
  6.4 0.8 copy-done.4
  7.2 0.0 copy-start.5
  7.2 0.7 copy-done.5
  7.9 0.0 copy-start.6
  7.9 0.7 copy-done.6
  8.5 46.4 %shard_map.113 = (bf16[1024,512]{1,0:T(8,128)(2,1)S(1)}, bf16[128,256]{1,0:T(8,128)(2,1)S(1)}, s32[1,32]{1,0:T(1,128)S(1)}) custom-call(s32[1,32]{1,0:T(1,128)S(1)} %bitcast.2, s32[1,32]{1,0:T(1,128)S(1)} %bitcast.3, bf16[1024,512]{1,0:T(8,128)(2,1)S(1)} %copy-done.1, bf16[128,256]{1,0:T(8,128)(2,1)S(1)} %copy-done.4, s32[32,32]{1,0:T(8,128)S(1)} %reshape.21.trow, ...), custom_call_target="tpu_custom_call" | custom-call | tf_op jit(solution)/shard_map/pallas_call | solution.py:353
  55.0 0.0 copy-start
  55.0 1.0 %copy-done = bf16[1024,512]{1,0:T(8,128)(2,1)} copy-done((bf16[1024,512]{1,0:T(8,128)(2,1)}, bf16[1024,512]{1,0:T(8,128)(2,1)S(1)}, u32[]{:S(2)}) %copy-start) | copy-done | bytes 1048600
  55.9 0.0 copy-start.7
  55.9 0.5 copy-done.7
  56.4 33.5 %shard_map.114 = bf16[1024,512]{1,0:T(8,128)(2,1)} custom-call(s32[1,32]{1,0:T(1,128)} %copy-done.7, bf16[1024,512]{1,0:T(8,128)(2,1)} %copy-done), custom_call_target="tpu_custom_call" | custom-call | tf_op jit(solution)/shard_map/pallas_call | solution.py:400
  90.0 0.6 copy.13
Async XLA Ops:
  2.9 1.2 %copy-start.1 = (bf16[1024,512]{1,0:T(8,128)(2,1)S(1)}, bf16[1024,512]{1,0:T(8,128)(2,1)}, u32[]{:S(2)}) copy-start(bf16[1024,512]{1,0:T(8,128)(2,1)} %edge_hbm.1) | copy-start | bytes 3145732
  4.1 1.2 %copy-start.2 = (bf16[2,2,256,512]{3,2,1,0:T(8,128)(2,1)S(1)}, bf16[2,2,256,512]{3,2,1,0:T(8,128)(2,1)}, u32[]{:S(2)}) copy-start(bf16[2,2,256,512]{3,2,1,0:T(8,128)(2,1)} %aw_hbm.1) | copy-start | bytes 3145732
  5.4 1.0 %copy-start.3 = (bf16[2,512,256]{2,1,0:T(8,128)(2,1)S(1)}, bf16[2,512,256]{2,1,0:T(8,128)(2,1)}, u32[]{:S(2)}) copy-start(bf16[2,512,256]{2,1,0:T(8,128)(2,1)} %ow_hbm.1) | copy-start | bytes 1572868
  6.4 0.8 copy-start.4
  7.2 0.7 copy-start.5
  7.9 0.7 copy-start.6
  55.0 1.0 %copy-start = (bf16[1024,512]{1,0:T(8,128)(2,1)}, bf16[1024,512]{1,0:T(8,128)(2,1)S(1)}, u32[]{:S(2)}) copy-start(bf16[1024,512]{1,0:T(8,128)(2,1)S(1)} %get-tuple-element.6.src) | copy-start | bytes 3145732
  55.9 0.5 copy-start.7

commit v2 on v1

--- a/solution.py
+++ b/solution.py
@@ -33,22 +33,27 @@
 
 def kernel(
     n,
+    rblock_hbm,
+    batom_hbm,
+    edge_hbm,
+    atom_hbm,
+    trow_hbm,
+    rlane_hbm,
+    satom_hbm,
+    ew_hbm,
+    aw_hbm,
+    ow_hbm,
+    edges,
+    atom_out,
+    pos_out,
     rblock,
     batom,
-    edge_hbm,
     atom_in,
     trow,
     rlane,
     satom,
-    ew_hbm,
-    aw_hbm,
-    ow_hbm,
-    edge_out,
-    atom_out,
-    pos_out,
     raw,
     ohe,
-    edges,
     upd,
     part,
     oht,
@@ -62,7 +67,6 @@
     aw,
     ow,
     load_sem,
-    out_sem,
     ag_send,
     ag_recv,
     x_send,
@@ -78,10 +82,20 @@
     has_up = me < n - 1
     has_dn = me > 0
 
-    loads = [pltpu.make_async_copy(edge_hbm, raw, load_sem.at[0])]
-    order = [(aw_hbm, aw, 0), (ew_hbm, ew, 0), (ow_hbm, ow, 0), (aw_hbm, aw, 1), (ew_hbm, ew, 1), (ow_hbm, ow, 1)]
-    for i, (src, dst, l) in enumerate(order):
-        loads.append(pltpu.make_async_copy(src.at[l], dst.at[l], load_sem.at[i + 1]))
+    order = [
+        (atom_hbm, atom_in),
+        (rblock_hbm, rblock),
+        (batom_hbm, batom),
+        (trow_hbm, trow),
+        (rlane_hbm, rlane),
+        (satom_hbm, satom),
+        (edge_hbm, raw),
+    ]
+    for l in range(LAYERS):
+        order += [(aw_hbm.at[l], aw.at[l]), (ew_hbm.at[l], ew.at[l]), (ow_hbm.at[l], ow.at[l])]
+    loads = []
+    for i, (src, dst) in enumerate(order):
+        loads.append(pltpu.make_async_copy(src, dst, load_sem.at[i]))
     for cp in loads:
         cp.start()
 
@@ -163,10 +177,13 @@
         here = pos == subs
         pcol = jnp.sum(jnp.where(here, lanes, 0), axis=1, keepdims=True)
         bcol = jnp.sum(jnp.where(here, jnp.broadcast_to(batom[...], square), 0), axis=1, keepdims=True)
-        pick = jnp.where(here, 1.0, 0.0).astype(BF16)
+        per_row = 128 // NB
+        pick = hot(pcol == per_row * (lanes % 8) + lanes // 8)
 
         def by_slot(ref):
-            return dot(pick, ref[...].astype(F32).astype(BF16)).T.astype(jnp.int32)
+            flat = ref[...].astype(F32)
+            blocks = jnp.concatenate([flat[:, j * NB : (j + 1) * NB] for j in range(per_row)], axis=0)
+            return dot(pick, blocks.astype(BF16)).T.astype(jnp.int32)
 
         tcol = by_slot(trow)
         scol = by_slot(satom)
@@ -195,25 +212,25 @@
             ohc[pl.ds(p * ATB, ATB), :] = hot(from_atom == bcol[p : p + 1, :] * ATB)
 
     def sort_edges():
-        loads[0].wait()
+        loads[6].wait()
         for q in range(4):
             rows = pl.ds(q * CH, CH)
             edges[rows, :] = dot(ohe[rows, :], raw[...]).astype(BF16)
 
-    def result(q):
-        rows = pl.ds(q * CH, CH)
-        return pltpu.make_async_copy(edges.at[rows], edge_out.at[rows], out_sem.at[q])
-
     for l in range(LAYERS):
         atoms = atom_in if l == 0 else atom_out
         del sent[:]
+        if l == 0:
+            loads[0].wait()
         table[l, shard_rows(me), :] = atoms[...]
+        push(l, me, y_peer)
         for d in range(1, planes):
             push(l, me, (me + 4 * d) % n)
-        push(l, me, y_peer)
         push(l, me, s_peer)
 
         if l == 0:
+            for cp in loads[1:6]:
+                cp.wait()
             prepare()
         for d in range(1, planes):
             shard = (me + n - 4 * d) % n
@@ -222,8 +239,8 @@
             push(l, shard, s_peer)
         if l == 0:
             sort_edges()
-            loads[1].wait()
-            loads[2].wait()
+            loads[7].wait()
+            loads[8].wait()
         for d in range(planes):
             shard = (y_peer + n - 4 * d) % n
             arrived(l, shard)
@@ -265,7 +282,7 @@
         first(3)
 
         if l == 0:
-            loads[3].wait()
+            loads[9].wait()
 
         def second(q, partner):
             rows = pl.ds(q * CH, CH)
@@ -274,8 +291,6 @@
             g = silu(dot(paired, ew[l, 2])).astype(BF16)
             e = (u + dot(g, ew[l, 3])).astype(BF16)
             edges[rows, :] = e
-            if l == LAYERS - 1:
-                result(q).start()
             return lax.dot_general(ohs[rows, :], e, (((0,), (0,)), ((), ())), preferred_element_type=F32)
 
         summed = second(2, upd[pl.ds(2 * CH, CH), :])
@@ -316,18 +331,19 @@
             exchange(l, False).wait_send()
 
         if l == 0:
-            for cp in loads[4:]:
+            for cp in loads[10:]:
                 cp.wait()
 
-    for q in range(4):
-        result(q).wait()
-
-
-def unsort(pos, src, dst, sem):
+
+def unsort(pos_in, src, atoms, dst, atoms_dst, pos, sem, atom_sem):
+    keep = pltpu.make_async_copy(atoms, atoms_dst, atom_sem)
+    keep.start()
+    pltpu.sync_copy(pos_in, pos)
     for b in range(EBLK):
         start = pl.multiple_of(pos[0, b] * NB, NB)
         pltpu.make_async_copy(src.at[pl.ds(start, NB)], dst.at[pl.ds(b * NB, NB)], sem).start()
     pltpu.make_async_copy(src, dst, sem).wait()
+    keep.wait()
 
 
 def local(
@@ -347,8 +363,7 @@
     da = atom_state.shape[1]
     e_dev = edge_state.shape[0]
     vmem = pl.BlockSpec(memory_space=pltpu.VMEM)
-    smem = pl.BlockSpec(memory_space=pltpu.SMEM)
-    anys = pl.BlockSpec(memory_space=pl.ANY)
+    hbm = pl.BlockSpec(memory_space=pltpu.HBM)
     planes = n // 4
     ordered, atoms, pos = pl.pallas_call(
         functools.partial(kernel, n),
@@ -357,12 +372,17 @@
             jax.ShapeDtypeStruct((A_DEV, da), BF16),
             jax.ShapeDtypeStruct((1, EBLK), jnp.int32),
         ),
-        in_specs=[vmem, vmem, anys, vmem, vmem, vmem, vmem, anys, anys, anys],
-        out_specs=(anys, vmem, vmem),
+        in_specs=[hbm] * 10,
+        out_specs=(vmem, vmem, vmem),
         scratch_shapes=[
+            pltpu.VMEM((1, EBLK), jnp.int32),
+            pltpu.VMEM((1, EBLK), jnp.int32),
+            pltpu.VMEM((A_DEV, da), BF16),
+            pltpu.VMEM((8, e_dev // 8), jnp.int32),
+            pltpu.VMEM((8, e_dev // 8), jnp.int32),
+            pltpu.VMEM((8, e_dev // 8), jnp.int32),
             pltpu.VMEM((e_dev, de), BF16),
             pltpu.VMEM((e_dev, e_dev), BF16),
-            pltpu.VMEM((e_dev, de), BF16),
             pltpu.VMEM((e_dev, de), BF16),
             pltpu.VMEM((e_dev, de), F32),
             pltpu.VMEM((e_dev, CH), BF16),
@@ -375,36 +395,37 @@
             pltpu.VMEM(edge_weights.shape, BF16),
             pltpu.VMEM(atom_in_weights.shape, BF16),
             pltpu.VMEM(atom_out_weights.shape, BF16),
-            pltpu.SemaphoreType.DMA((7,)),
-            pltpu.SemaphoreType.DMA((4,)),
+            pltpu.SemaphoreType.DMA((13,)),
             pltpu.SemaphoreType.DMA((LAYERS, 4 * planes)),
             pltpu.SemaphoreType.DMA((LAYERS, n)),
             pltpu.SemaphoreType.DMA((LAYERS, 2)),
             pltpu.SemaphoreType.DMA((LAYERS, 2)),
         ],
         compiler_params=pltpu.CompilerParams(
-            collective_id=0, has_side_effects=True, vmem_limit_bytes=48 * 1024 * 1024
+            collective_id=0, has_side_effects=True, vmem_limit_bytes=62 * 1024 * 1024
         ),
     )(
         reverse_block.reshape(1, EBLK),
         block_atom.reshape(1, EBLK),
         edge_state,
         atom_state,
-        target_row.reshape(EBLK, NB),
-        reverse_lane.reshape(EBLK, NB),
-        source_atom.reshape(EBLK, NB),
+        target_row.reshape(8, e_dev // 8),
+        reverse_lane.reshape(8, e_dev // 8),
+        source_atom.reshape(8, e_dev // 8),
         edge_weights,
         atom_in_weights,
         atom_out_weights,
     )
-    edges = pl.pallas_call(
+    return pl.pallas_call(
         unsort,
-        out_shape=jax.ShapeDtypeStruct((e_dev, de), BF16),
-        in_specs=[smem, anys],
-        out_specs=anys,
-        scratch_shapes=[pltpu.SemaphoreType.DMA],
-    )(pos, ordered)
-    return edges, atoms
+        out_shape=(
+            jax.ShapeDtypeStruct((e_dev, de), BF16),
+            jax.ShapeDtypeStruct((A_DEV, da), BF16),
+        ),
+        in_specs=[vmem, vmem, vmem],
+        out_specs=(hbm, hbm),
+        scratch_shapes=[pltpu.SMEM((1, EBLK), jnp.int32), pltpu.SemaphoreType.DMA, pltpu.SemaphoreType.DMA],
+    )(pos, ordered, atoms)
 
 
 def solution(mesh):

time: 91 us -> 50.7 us (0.56)
  Pallas kernels: 79.9 us -> 49.9 us
  local copies, waits for them, and re-layouts: 10 us -> 0 us
    pallas_call x1, Pallas kernels: 33.5 us -> 2.73 us  [local(): pl.pallas_call(unsort, out_shape=(jax.ShapeDtypeStruct((e_dev, de), BF16)...]
    unnamed x17 -> x0, local copies, waits for them, and re-layouts: 7.74 us -> none
    reshape x3 -> x0, local copies, waits for them, and re-layouts: 2.27 us -> none  [the longest x1 0.76 us: local(): reverse_lane.reshape(EBLK, NB)]
where the time goes in v2:
time: 50.7 us; the launch traced here: 50.5 us
  Pallas kernels  49.9 us (98%)
  between operations  0.64 us (1%)
    pallas_call x1, Pallas kernels, local(): pl.pallas_call(functools.partial(kernel, n), out_shape=(jax.ShapeDtypeStr...  47.2 us
    pallas_call x1, Pallas kernels, local(): pl.pallas_call(unsort, out_shape=(jax.ShapeDtypeStruct((e_dev, de), BF16)...  2.73 us

profile of v2, /device:TPU:9, one launch (start us, length us, event | category | flops | bytes accessed | tf_op | source)
XLA Modules:
  0.0 50.5 jit_solution(8237439161587970994)
XLA Ops:
  0.6 47.2 %shard_map.113 = (bf16[1024,512]{1,0:T(8,128)(2,1)}, bf16[128,256]{1,0:T(8,128)(2,1)}, s32[1,32]{1,0:T(1,128)}) custom-call(s32[1,32]{1,0:T(1,128)} %bitcast.8, s32[1,32]{1,0:T(1,128)} %bitcast.9, bf16[1024,512]{1,0:T(8,128)(2,1)} %edge_hbm.1, bf16[128,256]{1,0:T(8,128)(2,1)} %atom_hbm.1, s32[8,128]{1,0:T(8,128)} %bitcast.5, s32[8,128]{1,0:T(8,128)} %bitcast.6, ...), custom_call_target="tpu_custom_call" | custom-call | tf_op jit(solution)/shard_map/pallas_call | solution.py:368
  47.8 2.7 %shard_map.114 = (bf16[1024,512]{1,0:T(8,128)(2,1)}, bf16[128,256]{1,0:T(8,128)(2,1)}) custom-call(s32[1,32]{1,0:T(1,128)} %get-tuple-element.5.pos_in, bf16[1024,512]{1,0:T(8,128)(2,1)} %get-tuple-element.6.src, bf16[128,256]{1,0:T(8,128)(2,1)} %get-tuple-element.7.atoms), custom_call_target="tpu_custom_call" | custom-call | tf_op jit(solution)/shard_map/pallas_call | solution.py:419

commit v3 on v2

--- a/solution.py
+++ b/solution.py
@@ -228,10 +228,18 @@
             push(l, me, (me + 4 * d) % n)
         push(l, me, s_peer)
 
+        def own_part():
+            sproj = dot(atoms[...], aw[l, 1]).astype(BF16)
+            for q in range(4):
+                rows = pl.ds(q * CH, CH)
+                part[rows, :] = dot(edges[rows, :], ew[l, 0]) + dot(ohs[rows, :], sproj)
+
         if l == 0:
             for cp in loads[1:6]:
                 cp.wait()
             prepare()
+        else:
+            own_part()
         for d in range(1, planes):
             shard = (me + n - 4 * d) % n
             arrived(l, shard)
@@ -246,10 +254,8 @@
             arrived(l, shard)
             push(l, shard, s_peer)
 
-        sproj = dot(atoms[...], aw[l, 1]).astype(BF16)
-        for q in range(4):
-            rows = pl.ds(q * CH, CH)
-            part[rows, :] = dot(edges[rows, :], ew[l, 0]) + dot(ohs[rows, :], sproj)
+        if l == 0:
+            own_part()
 
         for d in range(planes):
             arrived(l, (s_peer + n - 4 * d) % n)

time: 50.7 us -> 50 us (0.986)
  Pallas kernels: 49.9 us -> 48.8 us
    pallas_call x1, Pallas kernels: 47.2 us -> 46.1 us  [local(): pl.pallas_call(functools.partial(kernel, n), out_shape=(jax.ShapeDtypeStr...]
where the time goes in v3:
time: 50 us; the launch traced here: 49.5 us
  Pallas kernels  48.8 us (98%)
  between operations  0.64 us (1%)
    pallas_call x1, Pallas kernels, local(): pl.pallas_call(functools.partial(kernel, n), out_shape=(jax.ShapeDtypeStr...  46.1 us
    pallas_call x1, Pallas kernels, local(): pl.pallas_call(unsort, out_shape=(jax.ShapeDtypeStruct((e_dev, de), BF16)...  2.73 us

profile of v3, /device:TPU:9, one launch (start us, length us, event | category | flops | bytes accessed | tf_op | source)
XLA Modules:
  0.0 49.5 jit_solution(16647320920420956879)
XLA Ops:
  0.6 46.1 %shard_map.113 = (bf16[1024,512]{1,0:T(8,128)(2,1)}, bf16[128,256]{1,0:T(8,128)(2,1)}, s32[1,32]{1,0:T(1,128)}) custom-call(s32[1,32]{1,0:T(1,128)} %bitcast.8, s32[1,32]{1,0:T(1,128)} %bitcast.9, bf16[1024,512]{1,0:T(8,128)(2,1)} %edge_hbm.1, bf16[128,256]{1,0:T(8,128)(2,1)} %atom_hbm.1, s32[8,128]{1,0:T(8,128)} %bitcast.5, s32[8,128]{1,0:T(8,128)} %bitcast.6, ...), custom_call_target="tpu_custom_call" | custom-call | tf_op jit(solution)/shard_map/pallas_call | solution.py:374
  46.7 2.7 %shard_map.114 = (bf16[1024,512]{1,0:T(8,128)(2,1)}, bf16[128,256]{1,0:T(8,128)(2,1)}) custom-call(s32[1,32]{1,0:T(1,128)} %get-tuple-element.5.pos_in, bf16[1024,512]{1,0:T(8,128)(2,1)} %get-tuple-element.6.src, bf16[128,256]{1,0:T(8,128)(2,1)} %get-tuple-element.7.atoms), custom_call_target="tpu_custom_call" | custom-call | tf_op jit(solution)/shard_map/pallas_call | solution.py:425
